TPU v7x, 256 devices: a whole 4x4x8 slice. The times are simulated.
256 devices in a mesh: dp: 16 (over y, z_hi, core), mp: 16 (over x, z_lo).
Axes of the slice: x: 4, y: 4, z: 8 (z_hi: 2, z_lo: 4; z = z_hi * 4 + z_lo), core: 2. Of those that a mesh axis runs over, the one named last changes fastest.
Arguments:
- skip_stream_arriving: float32 [4096, 2304], P('dp', 'mp'), may hold values from -170 to 170
- chosen_specialists: int32 [4096, 2], P('dp'), may hold values from 0 to 3, all different within a row; in each aligned block of 256 rows (0 to 255, 256 to 511, ...) at most 160 rows name the same one
- sequence_piece_tallies: int32 [16, 4], P('dp'), may hold values from 1 to 128, 256 in all within a row
- premix_rmsnorm_gain: float32 [2304], P('mp'), may hold values from 0.1 to 1.9
- dispatcher_weights: bfloat16 [2304, 4], replicated, may hold values from -0.125 to 0.125
- specialist_switch_weights: bfloat16 [4, 2304, 5760], P(None, 'dp', 'mp'), may hold values from -0.125 to 0.125
- specialist_expand_weights: bfloat16 [4, 2304, 5760], P(None, 'dp', 'mp'), may hold values from -0.125 to 0.125
- specialist_contract_weights: bfloat16 [4, 5760, 2304], P(None, 'mp', 'dp'), may hold values from -0.109375 to 0.109375
- terminal_rmsnorm_gain: float32 [2304], replicated, may hold values from 0.1 to 1.9
- lexicon_projector_weights: bfloat16 [2304, 131072], P(None, ('dp', 'mp')), may hold values from -12 to 12
- softness_per_sequence: float32 [64], replicated, may hold values from 0.02 to 1.5
Outputs:
- new_hidden: float32 [4096, 2304], P('dp', 'mp')
- logprobs: float32 [64, 131072], P(None, ('dp', 'mp'))
Inputs may be any that keep to these rules, and one draw needn't show every extreme that they name: `chosen_specialists`: in the 256 rows of each data group no expert is named by more than 160 rows, a bound that some block reaches. `sequence_piece_tallies`: each row sums to 256; its largest entry is 128.
All inputs are finite; a program needn't handle non-finite values.
Results may differ from a plain program's by a relative error of at most 0.0014.
Values may be sent and summed in bfloat16 or wider, within the bound.
A program may use at most 128 MiB of HBM per device.

v0:
```python
import math
import jax
import jax.numpy as jnp
from jax import lax
from jax.sharding import PartitionSpec as P

EMBED_DIMENSION = 2304
CAP = 160
branch_scale = 1.4 / math.sqrt(40.0)
epsilon = 1e-05


def slot_tables(routes_grp, expert, capacity):
    count = routes_grp.shape[0]
    hit = jnp.any(routes_grp == expert, axis=1)
    second = (routes_grp[:, 1] == expert).astype(jnp.int32)
    order = jnp.cumsum(hit.astype(jnp.int32), dtype=jnp.int32) - 1
    target = jnp.where(hit, order, capacity)
    tokens = jnp.arange(count, dtype=jnp.int32)
    slot_rows = jnp.zeros((capacity,), jnp.int32).at[target].set(tokens, mode="drop")
    live = jnp.zeros((capacity,), jnp.float32).at[target].set(1.0, mode="drop")
    which = jnp.zeros((capacity,), jnp.int32).at[target].set(second, mode="drop")
    return (slot_rows, live, which)


def body(
    skip_stream_arriving,
    chosen_specialists,
    sequence_piece_tallies,
    premix_rmsnorm_gain,
    dispatcher_weights,
    specialist_switch_weights,
    specialist_expand_weights,
    specialist_contract_weights,
    terminal_rmsnorm_gain,
    lexicon_projector_weights,
    softness_per_sequence,
):
    tok_rows = skip_stream_arriving.shape[0]
    local_width = skip_stream_arriving.shape[1]
    experts = specialist_switch_weights.shape[0]
    unit_cols = specialist_switch_weights.shape[2]
    squares = lax.psum(jnp.sum(skip_stream_arriving * skip_stream_arriving, axis=1), "mp")
    normed_local = (
        skip_stream_arriving
        * lax.rsqrt(squares / EMBED_DIMENSION + epsilon)[:, None]
        * premix_rmsnorm_gain
    ).astype(jnp.bfloat16)
    features = lax.all_gather(normed_local, "mp", axis=1, tiled=True)
    router = jnp.dot(features, dispatcher_weights, preferred_element_type=jnp.float32)
    mixing = jax.nn.softmax(jnp.take_along_axis(router, chosen_specialists, axis=1), axis=1)
    tables = [slot_tables(chosen_specialists, expert, CAP) for expert in range(experts)]
    inputs = jnp.stack([features[table[0]] for table in tables])
    scales = jnp.stack([mixing[table[0], table[2]] * table[1] for table in tables])
    pieces_out = []
    for expert in range(experts):
        rows_in = inputs[expert]

        def add_pair(carry, pieces, start, rows_in=rows_in):
            return (
                jnp.dot(rows_in, pieces[0], preferred_element_type=jnp.float32),
                jnp.dot(rows_in, pieces[1], preferred_element_type=jnp.float32),
            )

        empty = jnp.zeros((CAP, unit_cols), jnp.float32)
        gate, up_part = add_pair(
            (empty, empty),
            (
                lax.all_gather(specialist_switch_weights[expert], "dp", axis=0, tiled=True),
                lax.all_gather(specialist_expand_weights[expert], "dp", axis=0, tiled=True),
            ),
            jnp.int32(0),
        )
        act = (jax.nn.silu(gate) * up_part).astype(jnp.bfloat16)

        def project(piece, start, act=act):
            return jnp.dot(act, piece, preferred_element_type=jnp.float32)

        pieces_out.append(
            project(
                lax.all_gather(specialist_contract_weights[expert], "dp", axis=1, tiled=True),
                jnp.int32(0),
            )
        )
    outputs = jnp.stack(pieces_out)
    combined = jnp.zeros((tok_rows, EMBED_DIMENSION), jnp.float32)
    for expert in range(experts):
        combined = combined.at[tables[expert][0]].add(outputs[expert] * scales[expert][:, None])
    branch = lax.psum_scatter(
        combined.astype(jnp.bfloat16), "mp", scatter_dimension=1, tiled=True
    ).astype(jnp.float32)
    new_hidden = skip_stream_arriving + branch_scale * branch
    ends_index = jnp.cumsum(sequence_piece_tallies[0], dtype=jnp.int32) - 1
    end_local = new_hidden[ends_index]
    end_rows = lax.all_gather(end_local, "mp", axis=1, tiled=True)
    end_squares = jnp.sum(end_rows * end_rows, axis=1)
    end_normed = (
        end_rows
        * lax.rsqrt(end_squares / EMBED_DIMENSION + epsilon)[:, None]
        * terminal_rmsnorm_gain
    ).astype(jnp.bfloat16)
    lexicon_projector_feed = lax.all_gather(end_normed, "dp", axis=0, tiled=True)
    lexicon_logit_values = jnp.dot(
        lexicon_projector_feed, lexicon_projector_weights, preferred_element_type=jnp.float32
    ) / (EMBED_DIMENSION / 256.0 * softness_per_sequence[:, None])
    local_max = jnp.max(lexicon_logit_values, axis=1)
    local_sum = jnp.sum(jnp.exp(lexicon_logit_values - local_max[:, None]), axis=1)
    stats = jnp.stack([local_max, local_sum])
    for axis in ("mp", "dp"):
        held = lax.all_gather(stats, axis, axis=0)
        top = jnp.max(held[:, 0], axis=0)
        stats = jnp.stack([top, jnp.sum(held[:, 1] * jnp.exp(held[:, 0] - top[None]), axis=0)])
    largest, total_exp = (stats[0], stats[1])
    logprobs = lexicon_logit_values - largest[:, None] - jnp.log(total_exp)[:, None]
    return (new_hidden, logprobs)


def solution(mesh):
    return jax.shard_map(
        body,
        mesh=mesh,
        in_specs=(
            P("dp", "mp"),
            P("dp", None),
            P("dp", None),
            P("mp"),
            P(),
            P(None, "dp", "mp"),
            P(None, "dp", "mp"),
            P(None, "mp", "dp"),
            P(),
            P(None, ("dp", "mp")),
            P(),
        ),
        out_specs=(P("dp", "mp"), P(None, ("dp", "mp"))),
        check_vma=False,
    )
```

profile of v0, /device:TPU:1, one launch (start us, length us, event | category | flops | bytes accessed | tf_op | source)
XLA Modules:
  0.0 1087.2 jit_solution(11176963548852286973)
XLA Ops:
  8.4 38.4 %psum.7 = f32[256]{0:T(256)S(1)} all-reduce(f32[256]{0:T(256)S(1)} %multiply_reduce_fusion), channel_id=1, replica_groups=mesh['dp'=16,'mp'=16] {'mp'}, use_global_device_ids=true, to_apply=%region_5.6 | all-reduce | flops 256 | bytes 2048 | tf_op jit(solution)/shard_map/psum | solution.py:43
  83.7 43.5 %all-gather.33.cloned.1.call-done = bf16[256,2304]{0,1:T(8,128)(2,1)} async-done(((bf16[256,144]{0,1:T(8,128)(2,1)}), bf16[256,2304]{0,1:T(8,128)(2,1)}) %all-gather.33.cloned.1.call-update) | async-done | bytes 1179664 | tf_op jit(solution)/shard_map/all_gather | solution.py:49
  128.7 4.9 gather_fusion.9
  133.9 2.5 gather_fusion.3
  136.4 2.5 gather_fusion.1
  144.7 2.6 gather_fusion.5
  149.4 2.6 gather_fusion.7
  157.0 41.8 %all-gather.35.cloned.1.call-done = bf16[1,2304,360]{2,1,0:T(8,128)(2,1)} async-done(((bf16[1,144,360]{2,1,0:T(8,128)(2,1)}), bf16[1,2304,360]{2,1,0:T(8,128)(2,1)}) %all-gather.35.cloned.1.call-update) | async-done | bytes 1658896 | tf_op jit(solution)/shard_map/all_gather | solution.py:69
  201.0 56.7 %all-gather.37.cloned.1.call-done = bf16[1,2304,360]{2,1,0:T(8,128)(2,1)} async-done(((bf16[1,144,360]{2,1,0:T(8,128)(2,1)}), bf16[1,2304,360]{2,1,0:T(8,128)(2,1)}) %all-gather.37.cloned.1.call-update) | async-done | bytes 1658896 | tf_op jit(solution)/shard_map/all_gather | solution.py:70
  257.8 58.8 %all-gather.39.cloned.1.call-done = bf16[1,360,2304]{1,2,0:T(8,128)(2,1)} async-done(((bf16[1,360,144]{1,2,0:T(8,128)(2,1)}), bf16[1,360,2304]{1,2,0:T(8,128)(2,1)}) %all-gather.39.cloned.1.call-update) | async-done | bytes 1658896 | tf_op jit(solution)/shard_map/all_gather | solution.py:81
  316.6 4.4 convolution_multiply_fusion.3
  321.0 5.0 scatter_custom_fusion.3
  326.1 49.4 %all-gather.41.cloned.1.call-done = bf16[1,2304,360]{2,1,0:T(8,128)(2,1)} async-done(((bf16[1,144,360]{2,1,0:T(8,128)(2,1)}), bf16[1,2304,360]{2,1,0:T(8,128)(2,1)}) %all-gather.41.cloned.1.call-update) | async-done | bytes 1658896 | tf_op jit(solution)/shard_map/all_gather | solution.py:69
  377.4 56.8 %all-gather.43.cloned.1.call-done = bf16[1,2304,360]{2,1,0:T(8,128)(2,1)} async-done(((bf16[1,144,360]{2,1,0:T(8,128)(2,1)}), bf16[1,2304,360]{2,1,0:T(8,128)(2,1)}) %all-gather.43.cloned.1.call-update) | async-done | bytes 1658896 | tf_op jit(solution)/shard_map/all_gather | solution.py:70
  434.2 59.5 %all-gather.45.cloned.1.call-done = bf16[1,360,2304]{1,2,0:T(8,128)(2,1)} async-done(((bf16[1,360,144]{1,2,0:T(8,128)(2,1)}), bf16[1,360,2304]{1,2,0:T(8,128)(2,1)}) %all-gather.45.cloned.1.call-update) | async-done | bytes 1658896 | tf_op jit(solution)/shard_map/all_gather | solution.py:81
  493.8 4.4 convolution_multiply_fusion.2
  498.2 6.6 scatter_fusion
  504.7 48.0 %all-gather.47.cloned.1.call-done = bf16[1,2304,360]{2,1,0:T(8,128)(2,1)} async-done(((bf16[1,144,360]{2,1,0:T(8,128)(2,1)}), bf16[1,2304,360]{2,1,0:T(8,128)(2,1)}) %all-gather.47.cloned.1.call-update) | async-done | bytes 1658896 | tf_op jit(solution)/shard_map/all_gather | solution.py:69
  554.8 56.9 %all-gather.49.cloned.1.call-done = bf16[1,2304,360]{2,1,0:T(8,128)(2,1)} async-done(((bf16[1,144,360]{2,1,0:T(8,128)(2,1)}), bf16[1,2304,360]{2,1,0:T(8,128)(2,1)}) %all-gather.49.cloned.1.call-update) | async-done | bytes 1658896 | tf_op jit(solution)/shard_map/all_gather | solution.py:70
  611.8 58.8 %all-gather.51.cloned.1.call-done = bf16[1,360,2304]{1,2,0:T(8,128)(2,1)} async-done(((bf16[1,360,144]{1,2,0:T(8,128)(2,1)}), bf16[1,360,2304]{1,2,0:T(8,128)(2,1)}) %all-gather.51.cloned.1.call-update) | async-done | bytes 1658896 | tf_op jit(solution)/shard_map/all_gather | solution.py:81
  670.6 4.4 convolution_multiply_fusion.1
  675.0 6.6 scatter_fusion.1
  681.5 48.0 %all-gather.53.cloned.1.call-done = bf16[1,2304,360]{2,1,0:T(8,128)(2,1)} async-done(((bf16[1,144,360]{2,1,0:T(8,128)(2,1)}), bf16[1,2304,360]{2,1,0:T(8,128)(2,1)}) %all-gather.53.cloned.1.call-update) | async-done | bytes 1658896 | tf_op jit(solution)/shard_map/all_gather | solution.py:69
  731.6 56.8 %all-gather.55.cloned.1.call-done = bf16[1,2304,360]{2,1,0:T(8,128)(2,1)} async-done(((bf16[1,144,360]{2,1,0:T(8,128)(2,1)}), bf16[1,2304,360]{2,1,0:T(8,128)(2,1)}) %all-gather.55.cloned.1.call-update) | async-done | bytes 1658896 | tf_op jit(solution)/shard_map/all_gather | solution.py:70
  788.4 59.5 %all-gather.57.cloned.1.call-done = bf16[1,360,2304]{1,2,0:T(8,128)(2,1)} async-done(((bf16[1,360,144]{1,2,0:T(8,128)(2,1)}), bf16[1,360,2304]{1,2,0:T(8,128)(2,1)}) %all-gather.57.cloned.1.call-update) | async-done | bytes 1658896 | tf_op jit(solution)/shard_map/all_gather | solution.py:81
  848.0 4.3 convolution_multiply_fusion
  852.3 6.5 scatter_fusion.2
  863.3 70.4 %reduce-scatter.4.cloned.1.call-done = bf16[144,256]{1,0:T(8,128)(2,1)} async-done(((bf16[2304,256]{1,0:T(8,128)(2,1)}), bf16[144,256]{1,0:T(8,128)(2,1)}) %reduce-scatter.4.cloned.1.call-update) | async-done | bytes 73744
  936.1 31.2 %all-gather.15 = f32[16,144,4]{1,2,0:T(4,128)S(1)} all-gather(f32[1,144,4]{1,2,0:T(4,128)S(1)} %bitcast.132), channel_id=14, replica_groups=mesh['dp'=16,'mp'=16] {'mp'}, dimensions={0}, use_global_device_ids=true | all-gather | bytes 39168 | tf_op jit(solution)/shard_map/all_gather | solution.py:95
  967.7 50.6 %all-gather.16 = bf16[16,4,2304]{2,1,0:T(4,128)(2,1)S(1)} all-gather(bf16[1,4,2304]{2,1,0:T(4,128)(2,1)S(1)} %fusion.78), channel_id=1, replica_groups=mesh['dp'=16,'mp'=16] {'dp'}, dimensions={0}, use_global_device_ids=true | all-gather | bytes 313344 | tf_op jit(solution)/shard_map/all_gather | solution.py:102
  1019.2 29.8 %all-gather.17 = f32[16,2,64]{2,1,0:T(2,128)S(1)} all-gather(f32[1,2,64]{2,1,0:T(2,128)S(1)} %maximum_bitcast_fusion), channel_id=15, replica_groups=mesh['dp'=16,'mp'=16] {'mp'}, dimensions={0}, use_global_device_ids=true | all-gather | bytes 8704 | tf_op jit(solution)/shard_map/all_gather | solution.py:110
  1049.1 30.7 %all-gather.18 = f32[16,2,64]{2,1,0:T(2,128)S(1)} all-gather(f32[1,2,64]{2,1,0:T(2,128)S(1)} %maximum_bitcast_fusion.1), channel_id=16, replica_groups=mesh['dp'=16,'mp'=16] {'dp'}, dimensions={0}, use_global_device_ids=true | all-gather | bytes 8704 | tf_op jit(solution)/shard_map/all_gather | solution.py:110
  (172 shorter events, 69.6 us)
Async XLA Ops:
  7.2 1011.2 %copy-start = (bf16[2304,512]{1,0:T(8,128)(2,1)S(1)}, bf16[2304,512]{1,0:T(8,128)(2,1)}, u32[]{:S(2)}) copy-start(bf16[2304,512]{1,0:T(8,128)(2,1)} %param.20) | copy-start | bytes 7077892
  7.2 45.2 %copy-start.5 = (bf16[4,360,144]{1,2,0:T(8,128)(2,1)S(1)}, bf16[4,360,144]{1,2,0:T(8,128)(2,1)}, u32[]{:S(2)}) copy-start(bf16[4,360,144]{1,2,0:T(8,128)(2,1)} %param.18) | copy-start | bytes 1244164
  7.2 120.0 %all-gather.33.cloned.1.call-start = ((), (), s32[]{:S(2)}) async-start(), calls=%async_computation.1 | async-start | bytes 1253376 | tf_op jit(solution)/shard_map/all_gather | solution.py:49
  48.5 150.3 %all-gather.35.cloned.1.call-start = ((), (), s32[]{:S(2)}) async-start(), calls=%async_computation.2 | async-start | bytes 1880064 | tf_op jit(solution)/shard_map/all_gather | solution.py:69
  50.3 8.9 copy-start.6
  50.4 76.8 %copy-start.7 = (bf16[2304,4]{0,1:T(4,128)(2,1)S(1)}, bf16[2304,4]{0,1:T(4,128)(2,1)}, u32[]{:S(2)}) copy-start(bf16[2304,4]{0,1:T(4,128)(2,1)} %param.15) | copy-start | bytes 55300
  50.4 207.4 %all-gather.37.cloned.1.call-start = ((), (), s32[]{:S(2)}) async-start(), calls=%async_computation.3 | async-start | bytes 1880064 | tf_op jit(solution)/shard_map/all_gather | solution.py:70
  52.3 264.3 %all-gather.39.cloned.1.call-start = ((), (), s32[]{:S(2)}) async-start(), calls=%async_computation.4 | async-start | bytes 1880064 | tf_op jit(solution)/shard_map/all_gather | solution.py:81
  53.2 322.2 %all-gather.41.cloned.1.call-start = ((), (), s32[]{:S(2)}) async-start(), calls=%async_computation.5 | async-start | bytes 1880064 | tf_op jit(solution)/shard_map/all_gather | solution.py:69
  53.8 380.5 %all-gather.43.cloned.1.call-start = ((), (), s32[]{:S(2)}) async-start(), calls=%async_computation.6 | async-start | bytes 1880064 | tf_op jit(solution)/shard_map/all_gather | solution.py:70
  54.3 439.5 %all-gather.45.cloned.1.call-start = ((), (), s32[]{:S(2)}) async-start(), calls=%async_computation.7 | async-start | bytes 1880064 | tf_op jit(solution)/shard_map/all_gather | solution.py:81
  55.1 497.7 %all-gather.47.cloned.1.call-start = ((), (), s32[]{:S(2)}) async-start(), calls=%async_computation.8 | async-start | bytes 1880064 | tf_op jit(solution)/shard_map/all_gather | solution.py:69
  55.8 555.9 %all-gather.49.cloned.1.call-start = ((), (), s32[]{:S(2)}) async-start(), calls=%async_computation.9 | async-start | bytes 1880064 | tf_op jit(solution)/shard_map/all_gather | solution.py:70
  56.6 614.0 %all-gather.51.cloned.1.call-start = ((), (), s32[]{:S(2)}) async-start(), calls=%async_computation.10 | async-start | bytes 1880064 | tf_op jit(solution)/shard_map/all_gather | solution.py:81
  57.2 672.4 %all-gather.53.cloned.1.call-start = ((), (), s32[]{:S(2)}) async-start(), calls=%async_computation.11 | async-start | bytes 1880064 | tf_op jit(solution)/shard_map/all_gather | solution.py:69
  57.9 730.5 %all-gather.55.cloned.1.call-start = ((), (), s32[]{:S(2)}) async-start(), calls=%async_computation.12 | async-start | bytes 1880064 | tf_op jit(solution)/shard_map/all_gather | solution.py:70
  58.5 789.5 %all-gather.57.cloned.1.call-start = ((), (), s32[]{:S(2)}) async-start(), calls=%async_computation.13 | async-start | bytes 1880064 | tf_op jit(solution)/shard_map/all_gather | solution.py:81
  59.2 874.5 %reduce-scatter.4.cloned.1.call-start = ((), (), s32[]{:S(2)}) async-start(), calls=%async_computation.14 | async-start | bytes 1253376
  71.0 0.6 copy-start.15
  77.7 4.0 copy-start.11
  83.1 44.1 %copy-start.9 = (s32[160]{0:T(256)}, s32[160]{0:T(256)S(1)}, u32[]{:S(2)}) copy-start(s32[160]{0:T(256)S(1)} %get-tuple-element.37) | copy-start | bytes 1924
  152.0 2.2 copy-start.13
  152.0 3.0 copy-start.14
  154.2 162.4 %copy-start.4 = (bf16[160,2304]{1,0:T(8,128)(2,1)S(1)}, bf16[160,2304]{1,0:T(8,128)(2,1)}, u32[]{:S(2)}) copy-start(bf16[160,2304]{1,0:T(8,128)(2,1)} %gather_fusion) | copy-start | bytes 2211844
  321.0 54.4 %copy-start.3 = (bf16[160,2304]{1,0:T(8,128)(2,1)S(1)}, bf16[160,2304]{1,0:T(8,128)(2,1)}, u32[]{:S(2)}) copy-start(bf16[160,2304]{1,0:T(8,128)(2,1)} %gather_fusion.2) | copy-start | bytes 2211844
  498.2 54.6 %copy-start.2 = (bf16[160,2304]{1,0:T(8,128)(2,1)S(1)}, bf16[160,2304]{1,0:T(8,128)(2,1)}, u32[]{:S(2)}) copy-start(bf16[160,2304]{1,0:T(8,128)(2,1)} %gather_fusion.4) | copy-start | bytes 2211844
  554.8 120.2 %copy-start.12 = (s32[160]{0:T(256)S(1)}, s32[160]{0:T(256)}, u32[]{:S(2)}) copy-start(s32[160]{0:T(256)} %copy-done.11) | copy-start | bytes 1924
  675.0 54.6 %copy-start.1 = (bf16[160,2304]{1,0:T(8,128)(2,1)S(1)}, bf16[160,2304]{1,0:T(8,128)(2,1)}, u32[]{:S(2)}) copy-start(bf16[160,2304]{1,0:T(8,128)(2,1)} %gather_fusion.6) | copy-start | bytes 2211844
  731.6 120.7 %copy-start.10 = (s32[160]{0:T(256)S(1)}, s32[160]{0:T(256)}, u32[]{:S(2)}) copy-start(s32[160]{0:T(256)} %copy-done.9) | copy-start | bytes 1924
  860.6 2.5 copy-start.16
  860.6 2.7 copy-start.17
  862.0 105.6 %copy-start.8 = (f32[2304]{0:T(1024)S(1)}, f32[2304]{0:T(1024)}, u32[]{:S(2)}) copy-start(f32[2304]{0:T(1024)} %param.19) | copy-start | bytes 27652
Sparse Core Ops, SparseCore 0:
  48.6 78.5 all-gather.32
  129.8 68.9 all-gather.34
  201.4 56.3 all-gather.36
  260.2 56.3 all-gather.38
  319.0 56.3 all-gather.40
  377.9 56.3 all-gather.42
  437.4 56.3 all-gather.44
  496.4 56.3 all-gather.46
  555.4 56.3 all-gather.48
  614.2 56.3 all-gather.50
  673.2 56.3 all-gather.52
  732.0 56.3 all-gather.54
  791.6 56.3 all-gather.56
  862.2 71.5 reduce-scatter.3
where the time goes:
time: 1090 us
  waiting for transfers between devices  771 us (71%)
  blocking collectives  181 us (17%)
  local copies, waits for them, and re-layouts  55 us (5%)
  other arithmetic  37.7 us (3%)
  matrix products  28 us (3%)
  between operations  14.4 us (1%)
    all_gather x4, waiting for transfers between devices, body(): lax.all_gather(specialist_contract_weights[expert], 'dp', axis=1, tiled=T...  237 us
    all_gather x4, waiting for transfers between devices, body(): lax.all_gather(specialist_expand_weights[expert], 'dp', axis=0, tiled=True)  227 us
    all_gather x4, waiting for transfers between devices, body(): lax.all_gather(specialist_switch_weights[expert], 'dp', axis=0, tiled=True)  187 us
    unnamed x15, waiting for transfers between devices  76.1 us
    all_gather x2, blocking collectives, body(): held = lax.all_gather(stats, axis, axis=0)  60.5 us
    all_gather x1, blocking collectives, body(): lax.all_gather(end_normed, 'dp', axis=0, tiled=True)  50.6 us
    all_gather x1, waiting for transfers between devices, body(): features = lax.all_gather(normed_local, 'mp', axis=1, tiled=True)  43.5 us
    psum x1, blocking collectives, body(): lax.psum(jnp.sum(skip_stream_arriving * skip_stream_arriving, axis=1), 'mp')  38.4 us
  transfers between devices with their start and end apart: 14, of which 14 were waited for; matrix products, arithmetic and copies ran while one was open for 9% of the time, Pallas kernels for 0%

commit v1 on v0

--- a/solution.py
+++ b/solution.py
@@ -78,7 +78,15 @@
 
         pieces_out.append(
             project(
-                lax.all_gather(specialist_contract_weights[expert], "dp", axis=1, tiled=True),
+                jnp.concatenate(
+                    lax.all_to_all(
+                        jnp.stack([specialist_contract_weights[expert]] * lax.axis_size("dp")),
+                        "dp",
+                        0,
+                        0,
+                    ),
+                    axis=1,
+                ),
                 jnp.int32(0),
             )
         )

time: 1090 us -> 950 us (0.87)
  waiting for transfers between devices: 771 us -> 577 us
  starting transfers between devices: 0.55 us -> 33.9 us
  local copies, waits for them, and re-layouts: 55 us -> 68.8 us
    all_gather x4 -> x0, waiting for transfers between devices: 237 us -> none  [body(): lax.all_gather(specialist_contract_weights[expert], 'dp', axis=1, tiled=T...]
    all_to_all x0 -> x4, waiting for transfers between devices: none -> 98.5 us  [body(): lax.all_to_all(jnp.stack([specialist_contract_weights[expert]] * lax.axis...]
    all_gather x1, waiting for transfers between devices: 43.5 us -> 0.02 us  [body(): features = lax.all_gather(normed_local, 'mp', axis=1, tiled=True)]
    all_to_all x0 -> x4, starting transfers between devices: none -> 33.6 us  [body(): lax.all_to_all(jnp.stack([specialist_contract_weights[expert]] * lax.axis...]
    all_gather x4, waiting for transfers between devices: 187 us -> 162 us  [body(): lax.all_gather(specialist_switch_weights[expert], 'dp', axis=0, tiled=True)]
    all_gather x4, waiting for transfers between devices: 227 us -> 243 us  [body(): lax.all_gather(specialist_expand_weights[expert], 'dp', axis=0, tiled=True)]
    unnamed x15 -> x11, waiting for transfers between devices: 76.1 us -> 73.9 us
  transfers between devices with their start and end apart: 14 -> 14, of which waited for: 14 -> 12; matrix products, arithmetic and copies ran while one was open for 9% -> 12% of each run, Pallas kernels for 0% -> 0%
where the time goes in v1:
time: 950 us; the launch traced here: 941 us
  waiting for transfers between devices  577 us (61%)
  blocking collectives  181 us (19%)
  local copies, waits for them, and re-layouts  68.8 us (7%)
  other arithmetic  37.7 us (4%)
  starting transfers between devices  33.9 us (4%)
  matrix products  28 us (3%)
  between operations  15 us (2%)
    all_gather x4, waiting for transfers between devices, body(): lax.all_gather(specialist_expand_weights[expert], 'dp', axis=0, tiled=True)  243 us
    all_gather x4, waiting for transfers between devices, body(): lax.all_gather(specialist_switch_weights[expert], 'dp', axis=0, tiled=True)  162 us
    all_to_all x4, waiting for transfers between devices, body(): lax.all_to_all(jnp.stack([specialist_contract_weights[expert]] * lax.axis...  98.5 us
    unnamed x11, waiting for transfers between devices  73.9 us
    all_gather x2, blocking collectives, body(): held = lax.all_gather(stats, axis, axis=0)  60.6 us
    all_gather x1, blocking collectives, body(): lax.all_gather(end_normed, 'dp', axis=0, tiled=True)  50.6 us
    psum x1, blocking collectives, body(): lax.psum(jnp.sum(skip_stream_arriving * skip_stream_arriving, axis=1), 'mp')  38.4 us
    all_to_all x4, starting transfers between devices, body(): lax.all_to_all(jnp.stack([specialist_contract_weights[expert]] * lax.axis...  33.6 us
  transfers between devices with their start and end apart: 14, of which 12 were waited for; matrix products, arithmetic and copies ran while one was open for 12% of the time, Pallas kernels for 0%

profile of v1, /device:TPU:1, one launch (start us, length us, event | category | flops | bytes accessed | tf_op | source)
XLA Modules:
  0.0 941.2 jit_solution(1800277115857562482)
XLA Ops:
  8.4 38.4 %psum.7 = f32[256]{0:T(256)S(1)} all-reduce(f32[256]{0:T(256)S(1)} %multiply_reduce_fusion), channel_id=1, replica_groups=mesh['dp'=16,'mp'=16] {'mp'}, use_global_device_ids=true, to_apply=%region_5.6 | all-reduce | flops 256 | bytes 2048 | tf_op jit(solution)/shard_map/psum | solution.py:43
  56.2 16.3 %all-to-all-start.1 = ((bf16[16,360,144]{1,2,0:T(8,128)(2,1)}), bf16[16,360,144]{1,2,0:T(8,128)(2,1)}, u32[]{:S(2)}, u32[]{:S(2)}) async-start(bf16[16,360,144]{1,2,0:T(8,128)(2,1)} %stack.31), calls=%async_computation.1 | async-start | bytes 3538944 | tf_op jit(solution)/shard_map/all_to_all | solution.py:82
  73.2 54.7 %all-to-all-done.1 = bf16[16,360,144]{1,2,0:T(8,128)(2,1)} async-done(((bf16[16,360,144]{1,2,0:T(8,128)(2,1)}), bf16[16,360,144]{1,2,0:T(8,128)(2,1)}, u32[]{:S(2)}, u32[]{:S(2)}) %all-to-all-start.1) | async-done | bytes 1658912 | tf_op jit(solution)/shard_map/all_to_all | solution.py:82
  129.3 5.9 all-to-all-start
  137.2 40.5 %all-to-all-done = bf16[16,360,144]{1,2,0:T(8,128)(2,1)} async-done(((bf16[16,360,144]{1,2,0:T(8,128)(2,1)}), bf16[16,360,144]{1,2,0:T(8,128)(2,1)}, u32[]{:S(2)}, u32[]{:S(2)}) %all-to-all-start) | async-done | bytes 1658912 | tf_op jit(solution)/shard_map/all_to_all | solution.py:82
  179.1 4.8 all-to-all-start.2
  198.4 10.4 %scatter_custom_fusion.8 = s32[160]{0:T(256)S(1)} fusion(s32[256]{0:T(256)S(1)} %bitcast.168, s32[256]{0:T(256)S(1)} %iota.14, s32[]{:T(128)} %constant.26.clone.1), kind=kCustom, calls=%fused_computation.174 | custom fusion | bytes 644 | tf_op jit(solution)/shard_map/scatter | solution.py:20
  216.0 3.3 all-to-all-done.2
  220.7 6.5 all-to-all-start.3
  228.8 4.9 gather_fusion.9
  249.6 2.6 gather_fusion.7
  257.2 16.2 %all-gather.27.cloned.1.call-done = bf16[1,2304,360]{2,1,0:T(8,128)(2,1)} async-done(((bf16[1,144,360]{2,1,0:T(8,128)(2,1)}), bf16[1,2304,360]{2,1,0:T(8,128)(2,1)}) %all-gather.27.cloned.1.call-update) | async-done | bytes 1658896 | tf_op jit(solution)/shard_map/all_gather | solution.py:69
  275.7 70.9 %all-gather.29.cloned.1.call-done = bf16[1,2304,360]{2,1,0:T(8,128)(2,1)} async-done(((bf16[1,144,360]{2,1,0:T(8,128)(2,1)}), bf16[1,2304,360]{2,1,0:T(8,128)(2,1)}) %all-gather.29.cloned.1.call-update) | async-done | bytes 1658896 | tf_op jit(solution)/shard_map/all_gather | solution.py:70
  346.6 4.4 convolution_multiply_fusion.3
  351.0 5.0 scatter_custom_fusion.3
  356.0 49.4 %all-gather.31.cloned.1.call-done = bf16[1,2304,360]{2,1,0:T(8,128)(2,1)} async-done(((bf16[1,144,360]{2,1,0:T(8,128)(2,1)}), bf16[1,2304,360]{2,1,0:T(8,128)(2,1)}) %all-gather.31.cloned.1.call-update) | async-done | bytes 1658896 | tf_op jit(solution)/shard_map/all_gather | solution.py:69
  407.5 57.4 %all-gather.33.cloned.1.call-done = bf16[1,2304,360]{2,1,0:T(8,128)(2,1)} async-done(((bf16[1,144,360]{2,1,0:T(8,128)(2,1)}), bf16[1,2304,360]{2,1,0:T(8,128)(2,1)}) %all-gather.33.cloned.1.call-update) | async-done | bytes 1658896 | tf_op jit(solution)/shard_map/all_gather | solution.py:70
  464.8 4.4 convolution_multiply_fusion.2
  469.2 6.5 scatter_fusion
  475.8 47.9 %all-gather.35.cloned.1.call-done = bf16[1,2304,360]{2,1,0:T(8,128)(2,1)} async-done(((bf16[1,144,360]{2,1,0:T(8,128)(2,1)}), bf16[1,2304,360]{2,1,0:T(8,128)(2,1)}) %all-gather.35.cloned.1.call-update) | async-done | bytes 1658896 | tf_op jit(solution)/shard_map/all_gather | solution.py:69
  525.7 57.0 %all-gather.37.cloned.1.call-done = bf16[1,2304,360]{2,1,0:T(8,128)(2,1)} async-done(((bf16[1,144,360]{2,1,0:T(8,128)(2,1)}), bf16[1,2304,360]{2,1,0:T(8,128)(2,1)}) %all-gather.37.cloned.1.call-update) | async-done | bytes 1658896 | tf_op jit(solution)/shard_map/all_gather | solution.py:70
  582.6 4.5 convolution_multiply_fusion.1
  587.1 6.5 scatter_fusion.1
  593.7 48.0 %all-gather.39.cloned.1.call-done = bf16[1,2304,360]{2,1,0:T(8,128)(2,1)} async-done(((bf16[1,144,360]{2,1,0:T(8,128)(2,1)}), bf16[1,2304,360]{2,1,0:T(8,128)(2,1)}) %all-gather.39.cloned.1.call-update) | async-done | bytes 1658896 | tf_op jit(solution)/shard_map/all_gather | solution.py:69
  643.7 57.5 %all-gather.41.cloned.1.call-done = bf16[1,2304,360]{2,1,0:T(8,128)(2,1)} async-done(((bf16[1,144,360]{2,1,0:T(8,128)(2,1)}), bf16[1,2304,360]{2,1,0:T(8,128)(2,1)}) %all-gather.41.cloned.1.call-update) | async-done | bytes 1658896 | tf_op jit(solution)/shard_map/all_gather | solution.py:70
  701.2 4.4 convolution_multiply_fusion
  705.5 6.5 scatter_fusion.2
  716.6 70.1 %reduce-scatter.4.cloned.1.call-done = bf16[144,256]{1,0:T(8,128)(2,1)} async-done(((bf16[2304,256]{1,0:T(8,128)(2,1)}), bf16[144,256]{1,0:T(8,128)(2,1)}) %reduce-scatter.4.cloned.1.call-update) | async-done | bytes 73744
  789.0 31.6 %all-gather.11 = f32[16,144,4]{1,2,0:T(4,128)S(1)} all-gather(f32[1,144,4]{1,2,0:T(4,128)S(1)} %bitcast.144), channel_id=10, replica_groups=mesh['dp'=16,'mp'=16] {'mp'}, dimensions={0}, use_global_device_ids=true | all-gather | bytes 39168 | tf_op jit(solution)/shard_map/all_gather | solution.py:103
  821.0 50.6 %all-gather.12 = bf16[16,4,2304]{2,1,0:T(4,128)(2,1)S(1)} all-gather(bf16[1,4,2304]{2,1,0:T(4,128)(2,1)S(1)} %fusion.74), channel_id=1, replica_groups=mesh['dp'=16,'mp'=16] {'dp'}, dimensions={0}, use_global_device_ids=true | all-gather | bytes 313344 | tf_op jit(solution)/shard_map/all_gather | solution.py:110
  872.5 29.8 %all-gather.13 = f32[16,2,64]{2,1,0:T(2,128)S(1)} all-gather(f32[1,2,64]{2,1,0:T(2,128)S(1)} %maximum_bitcast_fusion), channel_id=11, replica_groups=mesh['dp'=16,'mp'=16] {'mp'}, dimensions={0}, use_global_device_ids=true | all-gather | bytes 8704 | tf_op jit(solution)/shard_map/all_gather | solution.py:118
  902.4 30.7 %all-gather.14 = f32[16,2,64]{2,1,0:T(2,128)S(1)} all-gather(f32[1,2,64]{2,1,0:T(2,128)S(1)} %maximum_bitcast_fusion.1), channel_id=12, replica_groups=mesh['dp'=16,'mp'=16] {'dp'}, dimensions={0}, use_global_device_ids=true | all-gather | bytes 8704 | tf_op jit(solution)/shard_map/all_gather | solution.py:118
  (172 shorter events, 78.6 us)
Async XLA Ops:
  7.2 864.5 %copy-start = (bf16[2304,512]{1,0:T(8,128)(2,1)S(1)}, bf16[2304,512]{1,0:T(8,128)(2,1)}, u32[]{:S(2)}) copy-start(bf16[2304,512]{1,0:T(8,128)(2,1)} %param.20) | copy-start | bytes 7077892
  7.2 47.6 %copy-start.5 = (bf16[4,360,144]{1,2,0:T(8,128)(2,1)S(1)}, bf16[4,360,144]{1,2,0:T(8,128)(2,1)}, u32[]{:S(2)}) copy-start(bf16[4,360,144]{1,2,0:T(8,128)(2,1)} %param.18) | copy-start | bytes 1244164
  7.2 220.0 %all-gather.25.cloned.1.call-start = ((), (), s32[]{:S(2)}) async-start(), calls=%async_computation.5 | async-start | bytes 1253376 | tf_op jit(solution)/shard_map/all_gather | solution.py:49
  48.5 225.0 %all-gather.27.cloned.1.call-start = ((), (), s32[]{:S(2)}) async-start(), calls=%async_computation.6 | async-start | bytes 1880064 | tf_op jit(solution)/shard_map/all_gather | solution.py:69
  50.4 296.2 %all-gather.29.cloned.1.call-start = ((), (), s32[]{:S(2)}) async-start(), calls=%async_computation.7 | async-start | bytes 1880064 | tf_op jit(solution)/shard_map/all_gather | solution.py:70
  52.3 353.2 %all-gather.31.cloned.1.call-start = ((), (), s32[]{:S(2)}) async-start(), calls=%async_computation.8 | async-start | bytes 1880064 | tf_op jit(solution)/shard_map/all_gather | solution.py:69
  52.9 412.0 %all-gather.33.cloned.1.call-start = ((), (), s32[]{:S(2)}) async-start(), calls=%async_computation.9 | async-start | bytes 1880064 | tf_op jit(solution)/shard_map/all_gather | solution.py:70
  53.4 470.2 %all-gather.35.cloned.1.call-start = ((), (), s32[]{:S(2)}) async-start(), calls=%async_computation.10 | async-start | bytes 1880064 | tf_op jit(solution)/shard_map/all_gather | solution.py:69
  54.0 528.6 %all-gather.37.cloned.1.call-start = ((), (), s32[]{:S(2)}) async-start(), calls=%async_computation.11 | async-start | bytes 1880064 | tf_op jit(solution)/shard_map/all_gather | solution.py:70
  56.2 71.7 %all-to-all-start.1 = ((bf16[16,360,144]{1,2,0:T(8,128)(2,1)}), bf16[16,360,144]{1,2,0:T(8,128)(2,1)}, u32[]{:S(2)}, u32[]{:S(2)}) async-start(bf16[16,360,144]{1,2,0:T(8,128)(2,1)} %stack.31), calls=%async_computation.1 | async-start | bytes 3538944 | tf_op jit(solution)/shard_map/all_to_all | solution.py:82
  72.5 569.1 %all-gather.39.cloned.1.call-start = ((), (), s32[]{:S(2)}) async-start(), calls=%async_computation.12 | async-start | bytes 1880064 | tf_op jit(solution)/shard_map/all_gather | solution.py:69
  129.3 6.7 copy-start.6
  129.3 48.5 %all-to-all-start = ((bf16[16,360,144]{1,2,0:T(8,128)(2,1)}), bf16[16,360,144]{1,2,0:T(8,128)(2,1)}, u32[]{:S(2)}, u32[]{:S(2)}) async-start(bf16[16,360,144]{1,2,0:T(8,128)(2,1)} %stack.30), calls=%async_computation | async-start | bytes 3538944 | tf_op jit(solution)/shard_map/all_to_all | solution.py:82
  135.2 566.0 %all-gather.41.cloned.1.call-start = ((), (), s32[]{:S(2)}) async-start(), calls=%async_computation.13 | async-start | bytes 1880064 | tf_op jit(solution)/shard_map/all_gather | solution.py:70
  179.1 40.2 %all-to-all-start.2 = ((bf16[16,360,144]{1,2,0:T(8,128)(2,1)}), bf16[16,360,144]{1,2,0:T(8,128)(2,1)}, u32[]{:S(2)}, u32[]{:S(2)}) async-start(bf16[16,360,144]{1,2,0:T(8,128)(2,1)} %stack.32), calls=%async_computation.2 | async-start | bytes 3538944 | tf_op jit(solution)/shard_map/all_to_all | solution.py:82
  213.6 0.6 copy-start.11
  214.2 6.4 copy-start.15
  214.8 5.8 copy-start.9
  220.7 6.6 copy-start.7
  220.7 423.0 %all-to-all-start.3 = ((bf16[16,360,144]{1,2,0:T(8,128)(2,1)}), bf16[16,360,144]{1,2,0:T(8,128)(2,1)}, u32[]{:S(2)}, u32[]{:S(2)}) async-start(bf16[16,360,144]{1,2,0:T(8,128)(2,1)} %stack.33), calls=%async_computation.3 | async-start | bytes 3538944 | tf_op jit(solution)/shard_map/all_to_all | solution.py:82
  227.2 559.5 %reduce-scatter.4.cloned.1.call-start = ((), (), s32[]{:S(2)}) async-start(), calls=%async_computation.14 | async-start | bytes 1253376
  252.2 2.2 copy-start.13
  252.2 3.0 copy-start.14
  254.4 92.2 %copy-start.4 = (bf16[160,2304]{1,0:T(8,128)(2,1)S(1)}, bf16[160,2304]{1,0:T(8,128)(2,1)}, u32[]{:S(2)}) copy-start(bf16[160,2304]{1,0:T(8,128)(2,1)} %gather_fusion) | copy-start | bytes 2211844
  351.0 54.5 %copy-start.3 = (bf16[160,2304]{1,0:T(8,128)(2,1)S(1)}, bf16[160,2304]{1,0:T(8,128)(2,1)}, u32[]{:S(2)}) copy-start(bf16[160,2304]{1,0:T(8,128)(2,1)} %gather_fusion.2) | copy-start | bytes 2211844
  464.8 4.4 copy-start.12
  469.2 54.5 %copy-start.2 = (bf16[160,2304]{1,0:T(8,128)(2,1)S(1)}, bf16[160,2304]{1,0:T(8,128)(2,1)}, u32[]{:S(2)}) copy-start(bf16[160,2304]{1,0:T(8,128)(2,1)} %gather_fusion.4) | copy-start | bytes 2211844
  582.6 4.5 copy-start.10
  587.1 54.5 %copy-start.1 = (bf16[160,2304]{1,0:T(8,128)(2,1)S(1)}, bf16[160,2304]{1,0:T(8,128)(2,1)}, u32[]{:S(2)}) copy-start(bf16[160,2304]{1,0:T(8,128)(2,1)} %gather_fusion.6) | copy-start | bytes 2211844
  713.8 2.5 copy-start.16
  713.8 2.7 copy-start.17
  715.3 105.7 %copy-start.8 = (f32[2304]{0:T(1024)S(1)}, f32[2304]{0:T(1024)}, u32[]{:S(2)}) copy-start(f32[2304]{0:T(1024)} %param.19) | copy-start | bytes 27652
Sparse Core Ops, SparseCore 0:
  48.6 119.7 all-gather.24
  171.0 102.4 all-gather.26
  276.1 70.4 all-gather.28
  349.1 56.3 all-gather.30
  408.5 56.3 all-gather.32
  467.3 56.3 all-gather.34
  526.3 56.3 all-gather.36
  585.3 56.3 all-gather.38
  644.8 56.3 all-gather.40
  715.4 71.2 reduce-scatter.3
